TPU v7x, 32 devices: a whole 2x2x4 slice. The times are simulated.
32 devices in a mesh: dp: 8 (over y, x, core), tp: 4 (over z).
Axes of the slice: x: 2, y: 2, z: 4, core: 2. Of those that a mesh axis runs over, the one named last changes fastest.
Arguments:
- tokens: bfloat16 [8, 512, 768], P('dp', 'tp'), may hold values from -6 to 6
- seg_ids: int32 [8, 512], P('dp'), may hold values from 0 to 2, never falling along the last dimension, each value on 1 to 256 neighbouring positions
- time_embed: float32 [8, 3, 768], P('dp'), may hold values from -6 to 6
- text_states: bfloat16 [8, 3, 64, 768], P('dp', None, 'tp'), may hold values from -6 to 6
- text_lengths: int32 [8, 3], P('dp'), may hold values from 16 to 64, as said below
- out_grad: bfloat16 [8, 512, 768], P('dp', 'tp'), may hold values from -6 to 6
- w_qkv: bfloat16 [768, 2304], P(None, 'tp'), may hold values from -0.21875 to 0.21875
- w_attn_out: bfloat16 [768, 768], P('tp'), may hold values from -3 to 3
- b_attn_out: bfloat16 [768], replicated, may hold values from -3 to 3
- w_cross_q: bfloat16 [768, 768], P(None, 'tp'), may hold values from -0.21875 to 0.21875
- w_cross_kv: bfloat16 [768, 1536], P(None, 'tp'), may hold values from -0.21875 to 0.21875
- w_cross_out: bfloat16 [768, 768], P('tp'), may hold values from -0.875 to 0.875
- b_cross_out: bfloat16 [768], replicated, may hold values from -3 to 3
- w_up: bfloat16 [768, 3072], P(None, 'tp'), may hold values from -0.21875 to 0.21875
- b_up: bfloat16 [3072], P('tp'), may hold values from -3 to 3
- w_down: bfloat16 [3072, 768], P('tp'), may hold values from -0.109375 to 0.109375
- w_mod: bfloat16 [768, 4608], P(None, 'tp'), may hold values from -0.21875 to 0.21875
- b_mod: bfloat16 [4608], P('tp'), may hold values from -3 to 3
Outputs:
- d_tokens: bfloat16 [8, 512, 768], P('dp', 'tp')
- d_time: float32 [8, 3, 768], P('dp')
- d_text: bfloat16 [8, 3, 64, 768], P('dp', None, 'tp')
- g_qkv: float32 [768, 2304], P(None, 'tp')
- g_attn_out: float32 [768, 768], P('tp')
- gb_attn_out: float32 [768], replicated
- g_cross_q: float32 [768, 768], P(None, 'tp')
- g_cross_kv: float32 [768, 1536], P(None, 'tp')
- g_cross_out: float32 [768, 768], P('tp')
- gb_cross_out: float32 [768], replicated
- g_up: float32 [768, 3072], P(None, 'tp')
- gb_up: float32 [3072], P('tp')
- g_down: float32 [3072, 768], P('tp')
- g_mod: float32 [768, 4608], P(None, 'tp')
- gb_mod: float32 [4608], P('tp')
Inputs may be any that keep to these rules, and one draw needn't show every extreme that they name: `seg_ids`: along a group's row item numbers never fall and every item of 0 to 2 has 1 to 256 frames. `text_lengths`: in every group one item has all 64 text tokens valid.
All inputs are finite; a program needn't handle non-finite values.
Results may differ from a plain program's by a relative error of at most 0.02.
Values may be sent and summed in bfloat16 or wider, within the bound.
A program may use at most 128 MiB of HBM per device.

v0:
```python
import math
import jax
import jax.numpy as jnp
from jax import lax
from jax.sharding import PartitionSpec as P

DH = 64


def dot_plain(left, right):
    return jnp.dot(left, right, preferred_element_type=jnp.float32)


def dot_left_t(left, right):
    return lax.dot_general(
        left, right, (((0,), (0,)), ((), ())), preferred_element_type=jnp.float32
    )


def dot_right_t(left, right):
    return lax.dot_general(
        left, right, (((1,), (1,)), ((), ())), preferred_element_type=jnp.float32
    )


def gelu_tanh(values):
    return jax.nn.gelu(values, approximate=True)


def normalize(values):
    center = values - jnp.mean(values, axis=-1, keepdims=True)
    inverse = lax.rsqrt(jnp.mean(center * center, axis=-1, keepdims=True) + 1e-06)
    return (center * inverse, inverse)


def normalize_back(grad, normed, inverse):
    return inverse * (
        grad
        - jnp.mean(grad, axis=-1, keepdims=True)
        - normed * jnp.mean(grad * normed, axis=-1, keepdims=True)
    )


def gather_rows(local_rows):
    return lax.all_gather(local_rows, "tp", axis=0, tiled=True)


def gather_grads(local_rows):
    return lax.all_gather(local_rows, "tp", axis=0, tiled=True)


def scatter_grads(full_rows):
    return lax.psum_scatter(full_rows, "tp", scatter_dimension=0, tiled=True)


def scatter_rows(attended, weight):
    return lax.psum_scatter(dot_plain(attended, weight), "tp", scatter_dimension=0, tiled=True)


def sum_bucket(first, second, third):
    return lax.psum((first, second, third), "dp")


def masked_scores(query_block, keys, tag_block, key_tag, scaling):
    scores = (
        jnp.einsum("rhd,khd->hrk", query_block, keys, preferred_element_type=jnp.float32) * scaling
    )
    return jnp.where((tag_block[:, None] == key_tag[None, :])[None], scores, -1000000000.0)


def attend_forward(query, keys, values, row_tag, key_tag, scaling):
    rows = query.shape[0]
    block_rows = min(512, rows)
    block_count = rows // block_rows

    def one_block(inputs):
        query_block, tag_block = inputs
        scores = masked_scores(query_block, keys, tag_block, key_tag, scaling)
        peak = jnp.max(scores, axis=-1, keepdims=True)
        exponent = jnp.exp(scores - peak)
        row_total = jnp.sum(exponent, axis=-1, keepdims=True)
        probs = (exponent / row_total).astype(jnp.bfloat16)
        result = jnp.einsum("hrk,khd->rhd", probs, values, preferred_element_type=jnp.float32)
        return (result, peak[..., 0] + jnp.log(row_total[..., 0]))

    result, log_total = lax.map(
        one_block,
        (
            query.reshape(block_count, block_rows, query.shape[1], query.shape[2]),
            row_tag.reshape(block_count, block_rows),
        ),
    )
    return (result.reshape(rows, -1), log_total)


def attend_backward(query, keys, values, row_tag, key_tag, scaling, log_total, d_result):
    rows = query.shape[0]
    block_rows = min(512, rows)
    block_count = rows // block_rows

    def one_block(carry, inputs):
        query_block, tag_block, total_block, grad_block = inputs
        scores = masked_scores(query_block, keys, tag_block, key_tag, scaling)
        probs = jnp.exp(scores - total_block[:, :, None])
        d_values = jnp.einsum(
            "hrk,rhd->khd",
            probs.astype(jnp.bfloat16),
            grad_block,
            preferred_element_type=jnp.float32,
        )
        d_probs = jnp.einsum("rhd,khd->hrk", grad_block, values, preferred_element_type=jnp.float32)
        d_scores = (probs * (d_probs - jnp.sum(probs * d_probs, axis=-1, keepdims=True))).astype(
            jnp.bfloat16
        )
        d_query = (
            jnp.einsum("hrk,khd->rhd", d_scores, keys, preferred_element_type=jnp.float32) * scaling
        )
        d_keys = (
            jnp.einsum("hrk,rhd->khd", d_scores, query_block, preferred_element_type=jnp.float32)
            * scaling
        )
        return ((carry[0] + d_keys, carry[1] + d_values), d_query)

    zeros = jnp.zeros(keys.shape, jnp.float32)
    shaped = (block_count, block_rows, query.shape[1], query.shape[2])
    (d_keys, d_values), d_query = lax.scan(
        one_block,
        (zeros, zeros),
        (
            query.reshape(shaped),
            row_tag.reshape(block_count, block_rows),
            log_total,
            d_result.reshape(shaped),
        ),
    )
    return (d_query.reshape(query.shape), d_keys, d_values)


def body(
    tokens,
    seg_ids,
    time_embed,
    text_states,
    text_lengths,
    out_grad,
    w_qkv,
    w_attn_out,
    b_attn_out,
    w_cross_q,
    w_cross_kv,
    w_cross_out,
    b_cross_out,
    w_up,
    b_up,
    w_down,
    w_mod,
    b_mod,
):
    shard_rows = tokens.shape[1]
    model_width = tokens.shape[2]
    item_count = time_embed.shape[1]
    scaling = 1.0 / math.sqrt(DH)
    heads_local = w_qkv.shape[1] // (3 * DH)
    tp_rank = lax.axis_index("tp")
    segment = seg_ids[0]
    frames = segment.shape[0]
    item_ids = jnp.arange(item_count, dtype=jnp.int32)
    local_segment = lax.dynamic_slice_in_dim(segment, tp_rank * shard_rows, shard_rows)
    onehot = (local_segment[:, None] == item_ids[None, :]).astype(jnp.float32)
    silu_time, silu_pull = jax.vjp(jax.nn.silu, time_embed[0])
    silu_low = silu_time.astype(jnp.bfloat16)
    mod_local = dot_plain(silu_low, w_mod) + b_mod.astype(jnp.float32)
    modulation = lax.all_gather(mod_local, "tp", axis=1, tiled=True)
    per_frame = jnp.dot(onehot, modulation, precision=lax.Precision.HIGHEST)
    shift_a, scale_a, gate_a, shift_m, scale_m, gate_m = jnp.split(per_frame, 6, axis=1)
    text_full = lax.all_gather(text_states[0], "tp", axis=1, tiled=True)
    text_count = text_full.shape[1]
    text_flat = text_full.reshape(item_count * text_count, model_width)
    key_index = jnp.arange(item_count * text_count, dtype=jnp.int32)
    key_item = key_index // text_count
    key_limit = jnp.sum(
        jnp.where(key_item[:, None] == item_ids[None, :], text_lengths[0][None, :], 0), axis=1
    )
    key_tag = jnp.where(key_index % text_count < key_limit, key_item, -1)
    stream_in = tokens[0].astype(jnp.float32)
    normed_a, inverse_a = normalize(stream_in)
    attn_in = gather_rows((normed_a * (1.0 + scale_a) + shift_a).astype(jnp.bfloat16))
    qkv = dot_plain(attn_in, w_qkv).astype(jnp.bfloat16).reshape(frames, heads_local, 3, DH)
    query, keys, values = (qkv[:, :, 0], qkv[:, :, 1], qkv[:, :, 2])
    attended, total_self = attend_forward(query, keys, values, segment, segment, scaling)
    attended = attended.astype(jnp.bfloat16)
    branch_a = scatter_rows(attended, w_attn_out) + b_attn_out.astype(jnp.float32)
    stream_a = stream_in + gate_a * branch_a
    normed_c, inverse_c = normalize(stream_a)
    cross_in = gather_rows(normed_c.astype(jnp.bfloat16))
    cross_query = (
        dot_plain(cross_in, w_cross_q).astype(jnp.bfloat16).reshape(frames, heads_local, DH)
    )
    cross_kv = (
        dot_plain(text_flat, w_cross_kv)
        .astype(jnp.bfloat16)
        .reshape(item_count * text_count, heads_local, 2, DH)
    )
    cross_keys, cross_values = (cross_kv[:, :, 0], cross_kv[:, :, 1])
    cross_attended, total_cross = attend_forward(
        cross_query, cross_keys, cross_values, segment, key_tag, scaling
    )
    cross_attended = cross_attended.astype(jnp.bfloat16)
    branch_c = scatter_rows(cross_attended, w_cross_out) + b_cross_out.astype(jnp.float32)
    stream_c = stream_a + branch_c
    normed_m, inverse_m = normalize(stream_c)
    mlp_in = gather_rows((normed_m * (1.0 + scale_m) + shift_m).astype(jnp.bfloat16))
    pre = dot_plain(mlp_in, w_up) + b_up.astype(jnp.float32)
    act, gelu_pull = jax.vjp(gelu_tanh, pre)
    act = act.astype(jnp.bfloat16)
    branch_m = scatter_rows(act, w_down)
    grad_out = out_grad[0].astype(jnp.float32)
    d_gate_m = grad_out * branch_m
    d_branch_m = gather_grads((grad_out * gate_m).astype(jnp.bfloat16))
    g_down = dot_left_t(act, d_branch_m)
    d_pre = gelu_pull(dot_right_t(d_branch_m, w_down))[0].astype(jnp.bfloat16)
    g_up = dot_left_t(mlp_in, d_pre)
    gb_up = jnp.sum(d_pre.astype(jnp.float32), axis=0)
    g_down, g_up, gb_up = sum_bucket(g_down, g_up, gb_up)
    d_mlp_in = scatter_grads(dot_right_t(d_pre, w_up))
    d_scale_m = d_mlp_in * normed_m
    grad_c = grad_out + normalize_back(d_mlp_in * (1.0 + scale_m), normed_m, inverse_m)
    d_branch_c = gather_grads(grad_c.astype(jnp.bfloat16))
    g_cross_out = dot_left_t(cross_attended, d_branch_c)
    gb_cross_out = jnp.sum(d_branch_c.astype(jnp.float32), axis=0)
    d_cross_result = (
        dot_right_t(d_branch_c, w_cross_out).astype(jnp.bfloat16).reshape(frames, heads_local, DH)
    )
    d_cross_query, d_cross_keys, d_cross_values = attend_backward(
        cross_query,
        cross_keys,
        cross_values,
        segment,
        key_tag,
        scaling,
        total_cross,
        d_cross_result,
    )
    d_cross_query = d_cross_query.reshape(frames, -1).astype(jnp.bfloat16)
    d_cross_kv = (
        jnp.stack([d_cross_keys, d_cross_values], axis=2)
        .reshape(item_count * text_count, -1)
        .astype(jnp.bfloat16)
    )
    g_cross_q = dot_left_t(cross_in, d_cross_query)
    g_cross_kv = dot_left_t(text_flat, d_cross_kv)
    g_cross_out, g_cross_q, g_cross_kv = sum_bucket(g_cross_out, g_cross_q, g_cross_kv)
    text_term = dot_right_t(d_cross_kv, w_cross_kv).reshape(item_count, text_count, model_width)
    d_text = lax.psum_scatter(text_term, "tp", scatter_dimension=1, tiled=True).astype(jnp.bfloat16)
    d_cross_in = scatter_grads(dot_right_t(d_cross_query, w_cross_q))
    grad_a = grad_c + normalize_back(d_cross_in, normed_c, inverse_c)
    d_gate_a = grad_a * branch_a
    d_branch_a = gather_grads((grad_a * gate_a).astype(jnp.bfloat16))
    g_attn_out = dot_left_t(attended, d_branch_a)
    gb_attn_out = jnp.sum(d_branch_a.astype(jnp.float32), axis=0)
    d_result = (
        dot_right_t(d_branch_a, w_attn_out).astype(jnp.bfloat16).reshape(frames, heads_local, DH)
    )
    d_query, d_keys, d_values = attend_backward(
        query, keys, values, segment, segment, scaling, total_self, d_result
    )
    d_qkv = jnp.stack([d_query, d_keys, d_values], axis=2).reshape(frames, -1).astype(jnp.bfloat16)
    g_qkv = dot_left_t(attn_in, d_qkv)
    g_attn_out, g_qkv, gb_attn_out = sum_bucket(g_attn_out, g_qkv, gb_attn_out)
    d_attn_in = scatter_grads(dot_right_t(d_qkv, w_qkv))
    d_scale_a = d_attn_in * normed_a
    d_tokens = (grad_a + normalize_back(d_attn_in * (1.0 + scale_a), normed_a, inverse_a)).astype(
        jnp.bfloat16
    )
    d_per_frame = jnp.concatenate(
        [d_attn_in, d_scale_a, d_gate_a, d_mlp_in, d_scale_m, d_gate_m], axis=1
    )
    d_mod_partial = jnp.dot(onehot.T, d_per_frame, precision=lax.Precision.HIGHEST)
    d_modulation = lax.psum_scatter(d_mod_partial, "tp", scatter_dimension=1, tiled=True).astype(
        jnp.bfloat16
    )
    g_mod = dot_left_t(silu_low, d_modulation)
    gb_mod = jnp.sum(d_modulation.astype(jnp.float32), axis=0)
    d_silu = lax.psum(dot_right_t(d_modulation, w_mod), "tp")
    d_time = silu_pull(d_silu)[0]
    g_mod, gb_mod, gb_cross_out = sum_bucket(g_mod, gb_mod, gb_cross_out)
    return (
        d_tokens[None],
        d_time[None],
        d_text[None],
        g_qkv,
        g_attn_out,
        gb_attn_out,
        g_cross_q,
        g_cross_kv,
        g_cross_out,
        gb_cross_out,
        g_up,
        gb_up,
        g_down,
        g_mod,
        gb_mod,
    )


def solution(mesh):
    placed = (
        P("dp", "tp", None),
        P("dp", None),
        P("dp", None, None),
        P("dp", None, "tp", None),
        P("dp", None),
        P("dp", "tp", None),
        P(None, "tp"),
        P("tp", None),
        P(),
        P(None, "tp"),
        P(None, "tp"),
        P("tp", None),
        P(),
        P(None, "tp"),
        P("tp"),
        P("tp", None),
        P(None, "tp"),
        P("tp"),
    )
    return jax.shard_map(
        body,
        mesh=mesh,
        in_specs=placed,
        out_specs=(
            P("dp", "tp", None),
            P("dp", None, None),
            P("dp", None, "tp", None),
            P(None, "tp"),
            P("tp", None),
            P(),
            P(None, "tp"),
            P(None, "tp"),
            P("tp", None),
            P(),
            P(None, "tp"),
            P("tp"),
            P("tp", None),
            P(None, "tp"),
            P("tp"),
        ),
        check_vma=False,
    )
```

profile of v0, /device:TPU:0, one launch (start us, length us, event | category | flops | bytes accessed | tf_op | source)
XLA Modules:
  0.0 679.7 jit_solution(6979725413255573108)
XLA Ops:
  11.3 15.1 %all_gather.24 = f32[3,4608]{1,0:T(4,128)S(1)} all-gather(f32[3,1152]{1,0:T(4,128)S(1)} %convolution_add_fusion), channel_id=1, replica_groups=mesh['dp'=8,'tp'=4] {'tp'}, dimensions={1}, use_global_device_ids=true | all-gather | bytes 69120 | tf_op jit(solution)/shard_map/all_gather | solution.py:173
  29.4 17.9 %all_gather.25 = bf16[512,768]{1,0:T(8,128)(2,1)S(1)} all-gather(bf16[128,768]{1,0:T(8,128)(2,1)S(1)} %fusion.42), channel_id=1, replica_groups=mesh['dp'=8,'tp'=4] {'tp'}, dimensions={0}, use_global_device_ids=true | all-gather | bytes 983040 | tf_op jit(solution)/shard_map/all_gather | solution.py:45
  53.7 15.6 %all-gather = bf16[1,3,64,768]{3,2,1,0:T(8,128)(2,1)S(1)} all-gather(bf16[1,3,16,768]{3,2,1,0:T(8,128)(2,1)S(1)} %copy-done.64), channel_id=2, replica_groups=mesh['dp'=8,'tp'=4] {'tp'}, dimensions={2}, use_global_device_ids=true | all-gather | bytes 368640 | tf_op jit(solution)/shard_map/all_gather | solution.py:176
  72.1 18.7 %reduce-scatter.11.cloned.1.call-done = f32[128,768]{1,0:T(8,128)} async-done(((f32[512,768]{1,0:T(8,128)}), f32[128,768]{1,0:T(8,128)}) %reduce-scatter.11.cloned.1.call-update) | async-done | bytes 393232 | tf_op jit(solution)/shard_map/reduce_scatter | solution.py:57
  92.4 17.6 %all_gather.27 = bf16[512,768]{1,0:T(8,128)(2,1)S(1)} all-gather(bf16[128,768]{1,0:T(8,128)(2,1)S(1)} %fusion.55), channel_id=1, replica_groups=mesh['dp'=8,'tp'=4] {'tp'}, dimensions={0}, use_global_device_ids=true | all-gather | bytes 983040 | tf_op jit(solution)/shard_map/all_gather | solution.py:45
  115.9 33.8 %reduce-scatter.13.cloned.1.call-done = f32[128,768]{1,0:T(8,128)} async-done(((f32[512,768]{1,0:T(8,128)}), f32[128,768]{1,0:T(8,128)}) %reduce-scatter.13.cloned.1.call-update) | async-done | bytes 393232 | tf_op jit(solution)/shard_map/reduce_scatter | solution.py:57
  152.6 18.2 %all_gather.28 = bf16[512,768]{1,0:T(8,128)(2,1)S(1)} all-gather(bf16[128,768]{1,0:T(8,128)(2,1)S(1)} %get-tuple-element.211), channel_id=1, replica_groups=mesh['dp'=8,'tp'=4] {'tp'}, dimensions={0}, use_global_device_ids=true | all-gather | bytes 983040 | tf_op jit(solution)/shard_map/all_gather | solution.py:49
  170.8 17.5 %all_gather.29 = bf16[512,768]{1,0:T(8,128)(2,1)S(1)} all-gather(bf16[128,768]{1,0:T(8,128)(2,1)S(1)} %get-tuple-element.212), channel_id=1, replica_groups=mesh['dp'=8,'tp'=4] {'tp'}, dimensions={0}, use_global_device_ids=true | all-gather | bytes 983040 | tf_op jit(solution)/shard_map/all_gather | solution.py:45
  189.9 3.4 convert_reduce_fusion
  196.9 34.3 %reduce-scatter.15.cloned.1.call-done = f32[128,768]{1,0:T(8,128)} async-done(((f32[512,768]{1,0:T(8,128)}), f32[128,768]{1,0:T(8,128)}) %reduce-scatter.15.cloned.1.call-update) | async-done | bytes 393232 | tf_op jit(solution)/shard_map/reduce_scatter | solution.py:53
  232.7 2.3 fusion.82
  235.0 18.5 %all_gather.30 = bf16[512,768]{1,0:T(8,128)(2,1)S(1)} all-gather(bf16[128,768]{1,0:T(8,128)(2,1)S(1)} %get-tuple-element.205), channel_id=1, replica_groups=mesh['dp'=8,'tp'=4] {'tp'}, dimensions={0}, use_global_device_ids=true | all-gather | bytes 983040 | tf_op jit(solution)/shard_map/all_gather | solution.py:49
  259.8 33.9 %reduce-scatter.17.cloned.1.call-done = f32[128,768]{1,0:T(8,128)} async-done(((f32[512,768]{1,0:T(8,128)}), f32[128,768]{1,0:T(8,128)}) %reduce-scatter.17.cloned.1.call-update) | async-done | bytes 393232 | tf_op jit(solution)/shard_map/reduce_scatter | solution.py:53
  295.0 2.3 multiply_convert_fusion.3
  297.4 18.1 %all_gather.31 = bf16[512,768]{1,0:T(8,128)(2,1)S(1)} all-gather(bf16[128,768]{1,0:T(8,128)(2,1)S(1)} %get-tuple-element.203), channel_id=1, replica_groups=mesh['dp'=8,'tp'=4] {'tp'}, dimensions={0}, use_global_device_ids=true | all-gather | bytes 983040 | tf_op jit(solution)/shard_map/all_gather | solution.py:49
  323.9 4.0 fusion.79
  328.0 3.9 fusion.96
  331.9 2.4 fusion.78
  337.8 20.7 %reduce-scatter.19.cloned.1.call-done = f32[128,768]{1,0:T(8,128)} async-done(((f32[512,768]{1,0:T(8,128)}), f32[128,768]{1,0:T(8,128)}) %reduce-scatter.19.cloned.1.call-update) | async-done | bytes 393232 | tf_op jit(solution)/shard_map/reduce_scatter | solution.py:53
  358.6 2.0 fusion.77
  360.6 2.1 fusion.48
  365.1 30.4 %reduce-scatter.21.cloned.1.call-done = f32[128,768]{1,0:T(8,128)} async-done(((f32[512,768]{1,0:T(8,128)}), f32[128,768]{1,0:T(8,128)}) %reduce-scatter.21.cloned.1.call-update) | async-done | bytes 393232 | tf_op jit(solution)/shard_map/reduce_scatter | solution.py:57
  397.3 5.1 convolution_bitcast_fusion
  404.8 2.5 fusion.98
  411.7 38.0 %reduce-scatter.25.cloned.1.call-done = f32[1152,3]{1,0:T(8,128)} async-done(((f32[4608,3]{1,0:T(8,128)}), f32[1152,3]{1,0:T(8,128)}) %reduce-scatter.25.cloned.1.call-update) | async-done | bytes 13840
  450.9 2.5 fusion.70
  453.6 20.4 %reduce-scatter.23.cloned.1.call-done = f32[3,16,768]{2,1,0:T(8,128)} async-done(((f32[3,64,768]{2,1,0:T(8,128)}), f32[3,16,768]{2,1,0:T(8,128)}) %reduce-scatter.23.cloned.1.call-update) | async-done | bytes 147472 | tf_op jit(solution)/shard_map/reduce_scatter | solution.py:254
  476.3 16.1 %psum.91 = f32[3,768]{1,0:T(4,128)S(1)} all-reduce(f32[3,768]{1,0:T(4,128)S(1)} %fusion.99), channel_id=1, replica_groups=mesh['dp'=8,'tp'=4] {'tp'}, use_global_device_ids=true, to_apply=%region_26.27 | all-reduce | flops 2304 | bytes 18432 | tf_op jit(solution)/shard_map/psum | solution.py:284
  493.1 24.7 %all-reduce = (f32[768]{0:T(1024)}, f32[768]{0:T(1024)}, f32[768]{0:T(1024)}, f32[1152]{0:T(1024)}) all-reduce(f32[768]{0:T(1024)S(1)} %convert_reduce_fusion.2, f32[768]{0:T(1024)S(1)} %convert_reduce_fusion.1, f32[768]{0:T(1024)S(1)} %copy-done.81, f32[1152]{0:T(1024)S(1)} %convert_reduce_fusion.4), channel_id=1, replica_groups=mesh['dp'=8,'tp'=4] {'dp'}, use_global_device_ids=true, to_apply=%region_31.32 | all-reduce | flops 3456 | bytes 27648 | tf_op jit(solution)/shard_map/psum | solution.py:61
  517.8 140.2 %all-reduce.4.cloned.1.call-done = (f32[768,576]{0,1:T(8,128)}, f32[192,768]{1,0:T(8,128)}, f32[768,192]{0,1:T(8,128)}, f32[768,384]{0,1:T(8,128)}, f32[192,768]...) async-done(((f32[768,576]{0,1:T(8,128)}, f32[192,768]{1,0:T(8,128)}, f32[768,192]{0,1:T(8,128)}, f32[768,384]{0,1:T(8,128)}, ...) | async-done | bytes 12976144 | tf_op jit(solution)/shard_map/psum | solution.py:61
  658.0 2.7 copy.88
  660.6 2.9 copy.133
  (293 shorter events, 77.2 us)
Async XLA Ops:
  7.2 19.2 %copy-start.70 = (s32[1,512]{1,0:T(1,128)S(1)}, s32[1,512]{1,0:T(1,128)}, u32[]{:S(2)}) copy-start(s32[1,512]{1,0:T(1,128)} %param.19) | copy-start | bytes 6148
  7.2 83.6 %reduce-scatter.11.cloned.1.call-start = ((), (), s32[]{:S(2)}) async-start(), calls=%async_computation.8 | async-start | bytes 1966080 | tf_op jit(solution)/shard_map/reduce_scatter | solution.py:57
  8.4 19.3 %copy-start.73 = (f32[128]{0:T(128)}, f32[128]{0:T(128)S(1)}, u32[]{:S(2)}) copy-start(f32[128]{0:T(128)S(1)} %broadcast_multiply_fusion.8) | copy-start | bytes 1540
  53.6 96.1 %reduce-scatter.13.cloned.1.call-start = ((), (), s32[]{:S(2)}) async-start(), calls=%async_computation.9 | async-start | bytes 1966080 | tf_op jit(solution)/shard_map/reduce_scatter | solution.py:57
  53.7 38.3 %copy-start.65 = (f32[768]{0:T(1024)}, f32[768]{0:T(1024)S(1)}, u32[]{:S(2)}) copy-start(f32[768]{0:T(1024)S(1)} %convert_element_type.171) | copy-start | bytes 9220
  72.1 37.9 %copy-start.43 = (bf16[768,192]{0,1:T(8,128)(2,1)S(1)}, bf16[768,192]{0,1:T(8,128)(2,1)}, u32[]{:S(2)}) copy-start(bf16[768,192]{0,1:T(8,128)(2,1)} %param.27) | copy-start | bytes 884740
  92.1 19.0 %copy-start.39 = (bf16[192,384]{0,1:T(8,128)(2,1)S(1)}, bf16[192,384]{0,1:T(8,128)(2,1)}, u32[]{:S(2)}) copy-start(bf16[192,384]{0,1:T(8,128)(2,1)} %copy.78) | copy-start | bytes 442372
  92.3 19.2 %copy-start.80 = (f32[128]{0:T(128)}, f32[128]{0:T(128)S(1)}, u32[]{:S(2)}) copy-start(f32[128]{0:T(128)S(1)} %add_rsqrt_fusion.1) | copy-start | bytes 1540
  114.6 116.6 %reduce-scatter.15.cloned.1.call-start = ((), (), s32[]{:S(2)}) async-start(), calls=%async_computation.10 | async-start | bytes 1966080 | tf_op jit(solution)/shard_map/reduce_scatter | solution.py:53
  150.8 19.9 %copy-start.4 = (f32[128,768]{1,0:T(8,128)}, f32[128,768]{1,0:T(8,128)S(1)}, u32[]{:S(2)}) copy-start(f32[128,768]{1,0:T(8,128)S(1)} %get-tuple-element.208) | copy-start | bytes 1179652
  150.9 19.9 %copy-start.71 = (f32[128]{0:T(128)}, f32[128]{0:T(128)S(1)}, u32[]{:S(2)}) copy-start(f32[128]{0:T(128)S(1)} %broadcast_multiply_fusion.6) | copy-start | bytes 1540
  151.1 19.7 %copy-start.76 = (f32[128]{0:T(128)}, f32[128]{0:T(128)S(1)}, u32[]{:S(2)}) copy-start(f32[128]{0:T(128)S(1)} %add_rsqrt_fusion) | copy-start | bytes 1540
  151.1 37.2 %copy-start.89 = (bf16[768,768]{1,0:T(8,128)(2,1)S(1)}, bf16[768,768]{1,0:T(8,128)(2,1)}, u32[]{:S(2)}) copy-start(bf16[768,768]{1,0:T(8,128)(2,1)} %param.33) | copy-start | bytes 3538948
  196.2 97.6 %reduce-scatter.17.cloned.1.call-start = ((), (), s32[]{:S(2)}) async-start(), calls=%async_computation.11 | async-start | bytes 1966080 | tf_op jit(solution)/shard_map/reduce_scatter | solution.py:53
  232.6 21.7 %copy-start.42 = (bf16[192,768]{1,0:T(8,128)(2,1)S(1)}, bf16[192,768]{1,0:T(8,128)(2,1)}, u32[]{:S(2)}) copy-start(bf16[192,768]{1,0:T(8,128)(2,1)} %param.29) | copy-start | bytes 884740
  235.0 19.8 %copy-start.40 = (bf16[192,384]{0,1:T(8,128)(2,1)S(1)}, bf16[192,384]{0,1:T(8,128)(2,1)}, u32[]{:S(2)}) copy-start(bf16[192,384]{0,1:T(8,128)(2,1)} %copy.78) | copy-start | bytes 442372
  259.0 99.5 %reduce-scatter.19.cloned.1.call-start = ((), (), s32[]{:S(2)}) async-start(), calls=%async_computation.12 | async-start | bytes 1966080 | tf_op jit(solution)/shard_map/reduce_scatter | solution.py:53
  293.8 22.7 %copy-start.46 = (bf16[192,768]{1,0:T(8,128)(2,1)S(1)}, bf16[192,768]{1,0:T(8,128)(2,1)}, u32[]{:S(2)}) copy-start(bf16[192,768]{1,0:T(8,128)(2,1)} %param.25) | copy-start | bytes 884740
  295.0 21.8 %copy-start.2 = (f32[3,512,512]{1,2,0:T(8,128)S(1)}, f32[3,512,512]{1,2,0:T(8,128)}, u32[]{:S(2)}) copy-start(f32[3,512,512]{1,2,0:T(8,128)} %copy-done.1) | copy-start | bytes 9437188
  323.9 71.7 %reduce-scatter.21.cloned.1.call-start = ((), (), s32[]{:S(2)}) async-start(), calls=%async_computation.13 | async-start | bytes 1966080 | tf_op jit(solution)/shard_map/reduce_scatter | solution.py:57
  327.9 121.8 %reduce-scatter.25.cloned.1.call-start = ((), (), s32[]{:S(2)}) async-start(), calls=%async_computation.15 | async-start | bytes 2949120
  335.0 23.5 %copy-start.74 = (f32[128]{0:T(128)S(1)}, f32[128]{0:T(128)}, u32[]{:S(2)}) copy-start(f32[128]{0:T(128)} %copy-done.73) | copy-start | bytes 1540
  335.0 23.5 %copy-start.79 = (f32[128]{0:T(128)S(1)}, f32[128]{0:T(128)}, u32[]{:S(2)}) copy-start(f32[128]{0:T(128)} %copy-done.78) | copy-start | bytes 1540
  336.6 23.9 %copy-start.19 = (f32[128,768]{1,0:T(8,128)S(1)}, f32[128,768]{1,0:T(8,128)}, u32[]{:S(2)}) copy-start(f32[128,768]{1,0:T(8,128)} %get-tuple-element.204) | copy-start | bytes 1179652
  337.8 24.9 %copy-start.37 = (f32[128,768]{1,0:T(8,128)S(1)}, f32[128,768]{1,0:T(8,128)}, u32[]{:S(2)}) copy-start(f32[128,768]{1,0:T(8,128)} %reduce-scatter.11.cloned.1.call-done) | copy-start | bytes 1179652
  337.8 24.9 %copy-start.66 = (f32[768]{0:T(1024)S(1)}, f32[768]{0:T(1024)}, u32[]{:S(2)}) copy-start(f32[768]{0:T(1024)} %copy-done.65) | copy-start | bytes 9220
  362.7 32.9 %copy-start.34 = (bf16[1,128,768]{2,1,0:T(8,128)(2,1)S(1)}, bf16[1,128,768]{2,1,0:T(8,128)(2,1)}, u32[]{:S(2)}) copy-start(bf16[1,128,768]{2,1,0:T(8,128)(2,1)} %param.23) | copy-start | bytes 589828
  363.5 33.9 %copy-start.86 = (s32[128]{0:T(128)S(1)}, s32[128]{0:T(128)}, u32[]{:S(2)}) copy-start(s32[128]{0:T(128)} %copy-done.85) | copy-start | bytes 1540
  402.5 71.5 %reduce-scatter.23.cloned.1.call-start = ((), (), s32[]{:S(2)}) async-start(), calls=%async_computation.14 | async-start | bytes 737280 | tf_op jit(solution)/shard_map/reduce_scatter | solution.py:254
  404.8 253.2 %all-reduce.4.cloned.1.call-start = ((), (), s32[]{:S(2)}) async-start(), calls=%async_computation.16 | async-start | bytes 25952256 | tf_op jit(solution)/shard_map/psum | solution.py:61
  409.8 41.1 %copy-start.63 = (f32[1,3,768]{2,0,1:T(1,128)S(1)}, f32[1,3,768]{2,0,1:T(1,128)}, u32[]{:S(2)}) copy-start(f32[1,3,768]{2,0,1:T(1,128)} %param.20) | copy-start | bytes 27652
  453.6 39.5 %copy-start.81 = (f32[768]{0:T(1024)S(1)}, f32[768]{0:T(1024)}, u32[]{:S(2)}) copy-start(f32[768]{0:T(1024)} %get-tuple-element.201) | copy-start | bytes 9220
  (68 other events, 262.3 us)
Sparse Core Ops, SparseCore 0:
  53.7 36.9 reduce-scatter.10
  114.7 34.9 reduce-scatter.12
  196.3 34.8 reduce-scatter.14
  259.2 34.5 reduce-scatter.16
  324.0 34.5 reduce-scatter.18
  361.3 34.2 reduce-scatter.20
  402.6 46.9 reduce-scatter.24
  452.5 21.4 reduce-scatter.22
  480.0 177.9 all-reduce.3
where the time goes:
time: 681 us; the launch traced here: 680 us
  waiting for transfers between devices  371 us (54%)
  blocking collectives  179 us (26%)
  matrix products  50.5 us (7%)
  local copies, waits for them, and re-layouts  34 us (5%)
  other arithmetic  30 us (4%)
  between operations  14.7 us (2%)
    psum x1, waiting for transfers between devices, sum_bucket(): return lax.psum((first, second, third), 'dp')  140 us
    reduce_scatter x3, waiting for transfers between devices, scatter_grads(): return lax.psum_scatter(full_rows, 'tp', scatter_dimension=0, tiled=True)  89 us
    reduce_scatter x3, waiting for transfers between devices, scatter_rows(): lax.psum_scatter(dot_plain(attended, weight), 'tp', scatter_dimension=0,...  82.9 us
    all_gather x3, blocking collectives, gather_grads(): return lax.all_gather(local_rows, 'tp', axis=0, tiled=True)  54.7 us
    all_gather x3, blocking collectives, gather_rows(): return lax.all_gather(local_rows, 'tp', axis=0, tiled=True)  53 us
    unnamed x10, waiting for transfers between devices  38.1 us
    unnamed x193, local copies, waits for them, and re-layouts  32.1 us
    psum x1, blocking collectives, sum_bucket(): return lax.psum((first, second, third), 'dp')  24.7 us
  transfers between devices with their start and end apart: 9, of which 9 were waited for; matrix products, arithmetic and copies ran while one was open for 6% of the time, Pallas kernels for 0%

commit v1 on v0

--- a/solution.py
+++ b/solution.py
@@ -5,6 +5,27 @@
 from jax.sharding import PartitionSpec as P
 
 DH = 64
+
+
+def collect(x, axis, dim):
+    devices, position, rows = (lax.axis_size(axis), lax.axis_index(axis), x.shape[dim])
+    forward = [(i, (i + 1) % devices) for i in range(devices)]
+    backward = [(i, (i - 1) % devices) for i in range(devices)]
+    out = jnp.zeros((*x.shape[:dim], devices * rows, *x.shape[dim + 1 :]), x.dtype)
+    out = lax.dynamic_update_slice_in_dim(out, x, position * rows, axis=dim)
+    from_left = from_right = x
+    half = devices // 2
+    for step in range(1, half + 1):
+        from_left = lax.ppermute(from_left, axis, forward)
+        out = lax.dynamic_update_slice_in_dim(
+            out, from_left, (position - step) % devices * rows, axis=dim
+        )
+        if step < devices - half:
+            from_right = lax.ppermute(from_right, axis, backward)
+            out = lax.dynamic_update_slice_in_dim(
+                out, from_right, (position + step) % devices * rows, axis=dim
+            )
+    return out
 
 
 def dot_plain(left, right):
@@ -173,7 +194,7 @@
     modulation = lax.all_gather(mod_local, "tp", axis=1, tiled=True)
     per_frame = jnp.dot(onehot, modulation, precision=lax.Precision.HIGHEST)
     shift_a, scale_a, gate_a, shift_m, scale_m, gate_m = jnp.split(per_frame, 6, axis=1)
-    text_full = lax.all_gather(text_states[0], "tp", axis=1, tiled=True)
+    text_full = collect(text_states[0], "tp", 1)
     text_count = text_full.shape[1]
     text_flat = text_full.reshape(item_count * text_count, model_width)
     key_index = jnp.arange(item_count * text_count, dtype=jnp.int32)

time: 681 us -> 679 us (level)
  blocking collectives: 179 us -> 164 us
  waiting for transfers between devices: 371 us -> 382 us
    all_gather x1 -> x0, blocking collectives: 15.6 us -> none  [body(): text_full = lax.all_gather(text_states[0], 'tp', axis=1, tiled=True)]
    ppermute x0 -> x3, waiting for transfers between devices: none -> 9.05 us  [the longest x2 9.04 us: collect(): from_left = lax.ppermute(from_left, axis, forward)]
    unnamed x193 -> x195, local copies, waits for them, and re-layouts: 32.1 us -> 30.1 us
  transfers between devices with their start and end apart: 9 -> 12, of which waited for: 9 -> 11; matrix products, arithmetic and copies ran while one was open for 6% -> 6% of each run, Pallas kernels for 0% -> 0%
where the time goes in v1:
time: 679 us; the launch traced here: 678 us
  waiting for transfers between devices  382 us (56%)
  blocking collectives  164 us (24%)
  matrix products  50.5 us (7%)
  local copies, waits for them, and re-layouts  32.2 us (5%)
  other arithmetic  30 us (4%)
  between operations  14.8 us (2%)
    psum x1, waiting for transfers between devices, sum_bucket(): return lax.psum((first, second, third), 'dp')  140 us
    reduce_scatter x3, waiting for transfers between devices, scatter_grads(): return lax.psum_scatter(full_rows, 'tp', scatter_dimension=0, tiled=True)  89.1 us
    reduce_scatter x3, waiting for transfers between devices, scatter_rows(): lax.psum_scatter(dot_plain(attended, weight), 'tp', scatter_dimension=0,...  84.8 us
    all_gather x3, blocking collectives, gather_grads(): return lax.all_gather(local_rows, 'tp', axis=0, tiled=True)  54.6 us
    all_gather x3, blocking collectives, gather_rows(): return lax.all_gather(local_rows, 'tp', axis=0, tiled=True)  53.6 us
    unnamed x10, waiting for transfers between devices  38 us
    unnamed x195, local copies, waits for them, and re-layouts  30.1 us
    psum x1, blocking collectives, sum_bucket(): return lax.psum((first, second, third), 'dp')  24.7 us
  transfers between devices with their start and end apart: 12, of which 11 were waited for; matrix products, arithmetic and copies ran while one was open for 6% of the time, Pallas kernels for 0%

profile of v1, /device:TPU:0, one launch (start us, length us, event | category | flops | bytes accessed | tf_op | source)
XLA Modules:
  0.0 677.8 jit_solution(13343750505361217308)
XLA Ops:
  11.3 15.1 %all_gather.21 = f32[3,4608]{1,0:T(4,128)S(1)} all-gather(f32[3,1152]{1,0:T(4,128)S(1)} %convolution_add_fusion), channel_id=1, replica_groups=mesh['dp'=8,'tp'=4] {'tp'}, dimensions={1}, use_global_device_ids=true | all-gather | bytes 69120 | tf_op jit(solution)/shard_map/all_gather | solution.py:194
  29.4 17.9 %all_gather.22 = bf16[512,768]{1,0:T(8,128)(2,1)S(1)} all-gather(bf16[128,768]{1,0:T(8,128)(2,1)S(1)} %fusion.42), channel_id=1, replica_groups=mesh['dp'=8,'tp'=4] {'tp'}, dimensions={0}, use_global_device_ids=true | all-gather | bytes 983040 | tf_op jit(solution)/shard_map/all_gather | solution.py:66
  53.9 3.6 collective-permute-start.1
  60.0 7.6 %collective-permute-done.2 = bf16[3,16,768]{2,1,0:T(8,128)(2,1)S(1)} collective-permute-done((bf16[3,16,768]{2,1,0:T(8,128)(2,1)S(1)}, bf16[3,16,768]{2,1,0:T(8,128)(2,1)S(1)}, u32[]{:S(2)}, u32[]{:S(2)}) %collective-permute-start.2) | collective-permute-done | bytes 73760 | tf_op jit(solution)/shard_map/ppermute | solution.py:19
  68.7 21.0 %reduce-scatter.11.cloned.1.call-done = f32[128,768]{1,0:T(8,128)} async-done(((f32[512,768]{1,0:T(8,128)}), f32[128,768]{1,0:T(8,128)}) %reduce-scatter.11.cloned.1.call-update) | async-done | bytes 393232 | tf_op jit(solution)/shard_map/reduce_scatter | solution.py:78
  91.4 18.1 %all_gather.23 = bf16[512,768]{1,0:T(8,128)(2,1)S(1)} all-gather(bf16[128,768]{1,0:T(8,128)(2,1)S(1)} %fusion.55), channel_id=1, replica_groups=mesh['dp'=8,'tp'=4] {'tp'}, dimensions={0}, use_global_device_ids=true | all-gather | bytes 983040 | tf_op jit(solution)/shard_map/all_gather | solution.py:66
  115.5 33.4 %reduce-scatter.13.cloned.1.call-done = f32[128,768]{1,0:T(8,128)} async-done(((f32[512,768]{1,0:T(8,128)}), f32[128,768]{1,0:T(8,128)}) %reduce-scatter.13.cloned.1.call-update) | async-done | bytes 393232 | tf_op jit(solution)/shard_map/reduce_scatter | solution.py:78
  151.8 18.2 %all_gather.24 = bf16[512,768]{1,0:T(8,128)(2,1)S(1)} all-gather(bf16[128,768]{1,0:T(8,128)(2,1)S(1)} %get-tuple-element.211), channel_id=1, replica_groups=mesh['dp'=8,'tp'=4] {'tp'}, dimensions={0}, use_global_device_ids=true | all-gather | bytes 983040 | tf_op jit(solution)/shard_map/all_gather | solution.py:70
  170.0 17.5 %all_gather.25 = bf16[512,768]{1,0:T(8,128)(2,1)S(1)} all-gather(bf16[128,768]{1,0:T(8,128)(2,1)S(1)} %get-tuple-element.212), channel_id=1, replica_groups=mesh['dp'=8,'tp'=4] {'tp'}, dimensions={0}, use_global_device_ids=true | all-gather | bytes 983040 | tf_op jit(solution)/shard_map/all_gather | solution.py:66
  189.1 3.4 convert_reduce_fusion
  196.1 34.3 %reduce-scatter.15.cloned.1.call-done = f32[128,768]{1,0:T(8,128)} async-done(((f32[512,768]{1,0:T(8,128)}), f32[128,768]{1,0:T(8,128)}) %reduce-scatter.15.cloned.1.call-update) | async-done | bytes 393232 | tf_op jit(solution)/shard_map/reduce_scatter | solution.py:74
  231.8 2.3 fusion.83
  234.1 18.4 %all_gather.26 = bf16[512,768]{1,0:T(8,128)(2,1)S(1)} all-gather(bf16[128,768]{1,0:T(8,128)(2,1)S(1)} %get-tuple-element.205), channel_id=1, replica_groups=mesh['dp'=8,'tp'=4] {'tp'}, dimensions={0}, use_global_device_ids=true | all-gather | bytes 983040 | tf_op jit(solution)/shard_map/all_gather | solution.py:70
  258.8 34.1 %reduce-scatter.17.cloned.1.call-done = f32[128,768]{1,0:T(8,128)} async-done(((f32[512,768]{1,0:T(8,128)}), f32[128,768]{1,0:T(8,128)}) %reduce-scatter.17.cloned.1.call-update) | async-done | bytes 393232 | tf_op jit(solution)/shard_map/reduce_scatter | solution.py:74
  294.2 2.3 multiply_convert_fusion.3
  296.5 18.1 %all_gather.27 = bf16[512,768]{1,0:T(8,128)(2,1)S(1)} all-gather(bf16[128,768]{1,0:T(8,128)(2,1)S(1)} %get-tuple-element.203), channel_id=1, replica_groups=mesh['dp'=8,'tp'=4] {'tp'}, dimensions={0}, use_global_device_ids=true | all-gather | bytes 983040 | tf_op jit(solution)/shard_map/all_gather | solution.py:70
  323.0 4.0 fusion.80
  327.1 3.9 fusion.98
  331.1 2.4 fusion.79
  336.9 20.8 %reduce-scatter.19.cloned.1.call-done = f32[128,768]{1,0:T(8,128)} async-done(((f32[512,768]{1,0:T(8,128)}), f32[128,768]{1,0:T(8,128)}) %reduce-scatter.19.cloned.1.call-update) | async-done | bytes 393232 | tf_op jit(solution)/shard_map/reduce_scatter | solution.py:74
  357.7 2.0 fusion.78
  359.8 2.1 fusion.48
  364.3 30.4 %reduce-scatter.21.cloned.1.call-done = f32[128,768]{1,0:T(8,128)} async-done(((f32[512,768]{1,0:T(8,128)}), f32[128,768]{1,0:T(8,128)}) %reduce-scatter.21.cloned.1.call-update) | async-done | bytes 393232 | tf_op jit(solution)/shard_map/reduce_scatter | solution.py:78
  396.5 5.1 convolution_bitcast_fusion
  404.0 2.5 fusion.100
  410.9 37.9 %reduce-scatter.25.cloned.1.call-done = f32[1152,3]{1,0:T(8,128)} async-done(((f32[4608,3]{1,0:T(8,128)}), f32[1152,3]{1,0:T(8,128)}) %reduce-scatter.25.cloned.1.call-update) | async-done | bytes 13840
  450.1 2.5 fusion.71
  452.8 20.3 %reduce-scatter.23.cloned.1.call-done = f32[3,16,768]{2,1,0:T(8,128)} async-done(((f32[3,64,768]{2,1,0:T(8,128)}), f32[3,16,768]{2,1,0:T(8,128)}) %reduce-scatter.23.cloned.1.call-update) | async-done | bytes 147472 | tf_op jit(solution)/shard_map/reduce_scatter | solution.py:275
  475.3 16.2 %psum.91 = f32[3,768]{1,0:T(4,128)S(1)} all-reduce(f32[3,768]{1,0:T(4,128)S(1)} %fusion.101), channel_id=1, replica_groups=mesh['dp'=8,'tp'=4] {'tp'}, use_global_device_ids=true, to_apply=%region_26.27 | all-reduce | flops 2304 | bytes 18432 | tf_op jit(solution)/shard_map/psum | solution.py:305
  492.2 24.7 %all-reduce = (f32[768]{0:T(1024)}, f32[768]{0:T(1024)}, f32[768]{0:T(1024)}, f32[1152]{0:T(1024)}) all-reduce(f32[768]{0:T(1024)S(1)} %convert_reduce_fusion.2, f32[768]{0:T(1024)S(1)} %convert_reduce_fusion.1, f32[768]{0:T(1024)S(1)} %copy-done.82, f32[1152]{0:T(1024)S(1)} %convert_reduce_fusion.4), channel_id=1, replica_groups=mesh['dp'=8,'tp'=4] {'dp'}, use_global_device_ids=true, to_apply=%region_31.32 | all-reduce | flops 3456 | bytes 27648 | tf_op jit(solution)/shard_map/psum | solution.py:82
  516.9 140.2 %all-reduce.4.cloned.1.call-done = (f32[768,576]{0,1:T(8,128)}, f32[192,768]{1,0:T(8,128)}, f32[768,192]{0,1:T(8,128)}, f32[768,384]{1,0:T(8,128)}, f32[192,768]...) async-done(((f32[768,576]{0,1:T(8,128)}, f32[192,768]{1,0:T(8,128)}, f32[768,192]{0,1:T(8,128)}, f32[768,384]{1,0:T(8,128)}, ...) | async-done | bytes 12976144 | tf_op jit(solution)/shard_map/psum | solution.py:82
  657.2 2.9 copy.133
  (305 shorter events, 79.8 us)
Async XLA Ops:
  7.2 82.6 %reduce-scatter.11.cloned.1.call-start = ((), (), s32[]{:S(2)}) async-start(), calls=%async_computation.8 | async-start | bytes 1966080 | tf_op jit(solution)/shard_map/reduce_scatter | solution.py:78
  53.6 95.3 %reduce-scatter.13.cloned.1.call-start = ((), (), s32[]{:S(2)}) async-start(), calls=%async_computation.9 | async-start | bytes 1966080 | tf_op jit(solution)/shard_map/reduce_scatter | solution.py:78
  53.6 6.3 collective-permute-start
  53.9 6.0 collective-permute-start.1
  58.4 32.6 %copy-start.66 = (f32[768]{0:T(1024)}, f32[768]{0:T(1024)S(1)}, u32[]{:S(2)}) copy-start(f32[768]{0:T(1024)S(1)} %convert_element_type.171) | copy-start | bytes 9220
  59.9 7.6 %collective-permute-start.2 = (bf16[3,16,768]{2,1,0:T(8,128)(2,1)S(1)}, bf16[3,16,768]{2,1,0:T(8,128)(2,1)S(1)}, u32[]{:S(2)}, u32[]{:S(2)}) collective-permute-start(bf16[3,16,768]{2,1,0:T(8,128)(2,1)S(1)} %collective-permute-done), channel_id=1, source_target_pairs={{0,1},{1,2},{2,3},{3,0},{4,5},{5,6},{6,7},{7,4},{8,9},{9,10},{10,1... | collective-permute-start | bytes 221192 | tf_op jit(solution)/shard_map/ppermute | solution.py:19
  67.6 23.7 %copy-start.22 = (bf16[3,64,768]{2,1,0:T(8,128)(2,1)}, bf16[3,64,768]{2,1,0:T(8,128)(2,1)S(1)}, u32[]{:S(2)}) copy-start(bf16[3,64,768]{2,1,0:T(8,128)(2,1)S(1)} %constant_dynamic-update-slice_fusion.2) | copy-start | bytes 884740
  68.7 40.8 %copy-start.44 = (bf16[768,192]{0,1:T(8,128)(2,1)S(1)}, bf16[768,192]{0,1:T(8,128)(2,1)}, u32[]{:S(2)}) copy-start(bf16[768,192]{0,1:T(8,128)(2,1)} %param.27) | copy-start | bytes 884740
  114.1 116.2 %reduce-scatter.15.cloned.1.call-start = ((), (), s32[]{:S(2)}) async-start(), calls=%async_computation.10 | async-start | bytes 1966080 | tf_op jit(solution)/shard_map/reduce_scatter | solution.py:74
  150.0 19.9 %copy-start.4 = (f32[128,768]{1,0:T(8,128)}, f32[128,768]{1,0:T(8,128)S(1)}, u32[]{:S(2)}) copy-start(f32[128,768]{1,0:T(8,128)S(1)} %get-tuple-element.208) | copy-start | bytes 1179652
  150.0 19.9 %copy-start.72 = (f32[128]{0:T(128)}, f32[128]{0:T(128)S(1)}, u32[]{:S(2)}) copy-start(f32[128]{0:T(128)S(1)} %broadcast_multiply_fusion.6) | copy-start | bytes 1540
  150.3 19.7 %copy-start.77 = (f32[128]{0:T(128)}, f32[128]{0:T(128)S(1)}, u32[]{:S(2)}) copy-start(f32[128]{0:T(128)S(1)} %add_rsqrt_fusion) | copy-start | bytes 1540
  150.3 37.2 %copy-start.90 = (bf16[768,768]{1,0:T(8,128)(2,1)S(1)}, bf16[768,768]{1,0:T(8,128)(2,1)}, u32[]{:S(2)}) copy-start(bf16[768,768]{1,0:T(8,128)(2,1)} %param.33) | copy-start | bytes 3538948
  195.3 97.6 %reduce-scatter.17.cloned.1.call-start = ((), (), s32[]{:S(2)}) async-start(), calls=%async_computation.11 | async-start | bytes 1966080 | tf_op jit(solution)/shard_map/reduce_scatter | solution.py:74
  231.8 21.6 %copy-start.43 = (bf16[192,768]{1,0:T(8,128)(2,1)S(1)}, bf16[192,768]{1,0:T(8,128)(2,1)}, u32[]{:S(2)}) copy-start(bf16[192,768]{1,0:T(8,128)(2,1)} %param.29) | copy-start | bytes 884740
  234.1 19.7 %copy-start.40 = (bf16[192,384]{0,1:T(8,128)(2,1)S(1)}, bf16[192,384]{0,1:T(8,128)(2,1)}, u32[]{:S(2)}) copy-start(bf16[192,384]{0,1:T(8,128)(2,1)} %copy.75) | copy-start | bytes 442372
  258.1 99.6 %reduce-scatter.19.cloned.1.call-start = ((), (), s32[]{:S(2)}) async-start(), calls=%async_computation.12 | async-start | bytes 1966080 | tf_op jit(solution)/shard_map/reduce_scatter | solution.py:74
  292.9 22.7 %copy-start.47 = (bf16[192,768]{1,0:T(8,128)(2,1)S(1)}, bf16[192,768]{1,0:T(8,128)(2,1)}, u32[]{:S(2)}) copy-start(bf16[192,768]{1,0:T(8,128)(2,1)} %param.25) | copy-start | bytes 884740
  294.2 21.8 %copy-start.2 = (f32[3,512,512]{1,2,0:T(8,128)S(1)}, f32[3,512,512]{1,2,0:T(8,128)}, u32[]{:S(2)}) copy-start(f32[3,512,512]{1,2,0:T(8,128)} %copy-done.1) | copy-start | bytes 9437188
  323.0 71.7 %reduce-scatter.21.cloned.1.call-start = ((), (), s32[]{:S(2)}) async-start(), calls=%async_computation.13 | async-start | bytes 1966080 | tf_op jit(solution)/shard_map/reduce_scatter | solution.py:78
  327.0 121.8 %reduce-scatter.25.cloned.1.call-start = ((), (), s32[]{:S(2)}) async-start(), calls=%async_computation.15 | async-start | bytes 2949120
  334.1 23.6 %copy-start.75 = (f32[128]{0:T(128)S(1)}, f32[128]{0:T(128)}, u32[]{:S(2)}) copy-start(f32[128]{0:T(128)} %copy-done.74) | copy-start | bytes 1540
  334.2 23.6 %copy-start.80 = (f32[128]{0:T(128)S(1)}, f32[128]{0:T(128)}, u32[]{:S(2)}) copy-start(f32[128]{0:T(128)} %copy-done.79) | copy-start | bytes 1540
  335.8 23.9 %copy-start.19 = (f32[128,768]{1,0:T(8,128)S(1)}, f32[128,768]{1,0:T(8,128)}, u32[]{:S(2)}) copy-start(f32[128,768]{1,0:T(8,128)} %get-tuple-element.204) | copy-start | bytes 1179652
  336.9 24.9 %copy-start.37 = (f32[128,768]{1,0:T(8,128)S(1)}, f32[128,768]{1,0:T(8,128)}, u32[]{:S(2)}) copy-start(f32[128,768]{1,0:T(8,128)} %reduce-scatter.11.cloned.1.call-done) | copy-start | bytes 1179652
  336.9 24.9 %copy-start.67 = (f32[768]{0:T(1024)S(1)}, f32[768]{0:T(1024)}, u32[]{:S(2)}) copy-start(f32[768]{0:T(1024)} %copy-done.66) | copy-start | bytes 9220
  361.8 32.9 %copy-start.34 = (bf16[1,128,768]{2,1,0:T(8,128)(2,1)S(1)}, bf16[1,128,768]{2,1,0:T(8,128)(2,1)}, u32[]{:S(2)}) copy-start(bf16[1,128,768]{2,1,0:T(8,128)(2,1)} %param.23) | copy-start | bytes 589828
  362.6 33.9 %copy-start.87 = (s32[128]{0:T(128)S(1)}, s32[128]{0:T(128)}, u32[]{:S(2)}) copy-start(s32[128]{0:T(128)} %copy-done.86) | copy-start | bytes 1540
  401.7 71.4 %reduce-scatter.23.cloned.1.call-start = ((), (), s32[]{:S(2)}) async-start(), calls=%async_computation.14 | async-start | bytes 737280 | tf_op jit(solution)/shard_map/reduce_scatter | solution.py:275
  403.9 253.2 %all-reduce.4.cloned.1.call-start = ((), (), s32[]{:S(2)}) async-start(), calls=%async_computation.16 | async-start | bytes 25952256 | tf_op jit(solution)/shard_map/psum | solution.py:82
  409.1 41.0 %copy-start.64 = (f32[1,3,768]{2,0,1:T(1,128)S(1)}, f32[1,3,768]{2,0,1:T(1,128)}, u32[]{:S(2)}) copy-start(f32[1,3,768]{2,0,1:T(1,128)} %param.20) | copy-start | bytes 27652
  452.8 39.4 %copy-start.82 = (f32[768]{0:T(1024)S(1)}, f32[768]{0:T(1024)}, u32[]{:S(2)}) copy-start(f32[768]{0:T(1024)} %get-tuple-element.201) | copy-start | bytes 9220
  (72 other events, 325.8 us)
Sparse Core Ops, SparseCore 0:
  53.7 36.0 reduce-scatter.10
  114.3 34.5 reduce-scatter.12
  195.4 34.8 reduce-scatter.14
  258.2 34.6 reduce-scatter.16
  323.1 34.5 reduce-scatter.18
  360.4 34.2 reduce-scatter.20
  401.8 46.9 reduce-scatter.24
  451.7 21.3 reduce-scatter.22
  479.0 178.0 all-reduce.3
